TPU v7x, 256 devices: a whole 4x4x8 slice. The times are simulated.
256 devices in a mesh: cluster: 32 (over z, y), group: 8 (over x, core).
Axes of the slice: x: 4, y: 4, z: 8, core: 2. Of those that a mesh axis runs over, the one named last changes fastest.
Arguments:
- loads: bfloat16 [512, 131072], P('group', 'cluster'), may hold values from -6 to 6
- near_blocks: bfloat16 [512, 24, 256, 256], P('cluster', 'group'), may hold values from -0.078125 to 0.078125
- near_cols: int32 [512, 24], P('cluster'), may hold values from 0 to 511, as said below
- far_right: bfloat16 [512, 64, 256], P('cluster'), may hold values from -0.375 to 0.375
- far_coupling: bfloat16 [512, 64, 1024], P('cluster'), may hold values from -0.1875 to 0.1875
- far_left: bfloat16 [512, 64, 256], P('cluster'), may hold values from -0.75 to 0.75
- far_cols: int32 [512, 16], P('cluster'), may hold values from 0 to 511, as said below
Outputs:
- response: bfloat16 [512, 131072], P('group', 'cluster')
Inputs may be any that keep to these rules, and one draw needn't show every extreme that they name: `near_cols`: the 24 entries of a row are distinct leaves i + d modulo 512, with |d| <= 16, for row leaf i. `far_cols`: the 16 entries of a row are distinct leaves i + d modulo 512, with 16 < d < 496, for row leaf i.
All inputs are finite; a program needn't handle non-finite values.
Results may differ from a plain program's by a relative error of at most 0.0049.
Values may be sent and summed in bfloat16 or wider, within the bound.
No kernel may reach another device: no remote copies, remote signals or barrier semaphores. Data moves between devices by JAX's collectives and lax.ppermute only.
A program may use at most 128 MiB of HBM per device.

v0:
```python
import jax
import jax.numpy as jnp
from jax import lax
from jax.sharding import PartitionSpec as P

REACH = 16


def with_halo(cells, sides, width):
    for axis, dim in sides:
        count = lax.axis_size(axis)
        head = lax.slice_in_dim(cells, 0, width, axis=dim)
        tail = lax.slice_in_dim(cells, cells.shape[dim] - width, cells.shape[dim], axis=dim)
        cells = jnp.concatenate(
            [
                lax.ppermute(tail, axis, [(i, (i + 1) % count) for i in range(count)]),
                cells,
                lax.ppermute(head, axis, [((i + 1) % count, i) for i in range(count)]),
            ],
            axis=dim,
        )
    return cells


def local(loads, near_blocks, near_cols, far_right, far_coupling, far_left, far_cols):
    columns = loads.shape[0]
    leaf_count = near_blocks.shape[0]
    per_group = near_blocks.shape[1]
    leaf = near_blocks.shape[2]
    rank = far_right.shape[1]
    far_count = far_cols.shape[1]
    total_leaves = leaf_count * lax.axis_size("cluster")
    cluster_id = lax.axis_index("cluster")
    group_id = lax.axis_index("group")
    gathered = lax.all_gather(loads, "group", axis=0, tiled=True)
    patterns = gathered.shape[0]
    widened = with_halo(gathered, (("cluster", 1),), REACH * leaf)
    wide_leaves = leaf_count + 2 * REACH
    wide_view = widened.reshape(patterns, wide_leaves, leaf)
    first_leaf = cluster_id * leaf_count - REACH
    leaf_ids = lax.dynamic_slice_in_dim(near_cols, group_id * per_group, per_group, 1)
    position = (leaf_ids - first_leaf) % total_leaves
    picked = jnp.take(wide_view, position, axis=1)
    result = jnp.einsum("rmkc,mknc->rmn", picked, near_blocks, preferred_element_type=jnp.float32)
    partial_value = result.reshape(patterns, near_blocks.shape[0] * leaf)
    near = lax.psum_scatter(partial_value, "group", scatter_dimension=0, tiled=True)
    own_loads = loads.reshape(columns, leaf_count, leaf)
    coef = jnp.einsum("rlc,lac->lra", own_loads, far_right, preferred_element_type=jnp.float32)
    coef = coef.astype(jnp.bfloat16).reshape(leaf_count, columns * rank)
    coupling = far_coupling.reshape(leaf_count, rank, far_count, rank)
    every_coef = lax.all_gather(coef, "cluster", axis=0, tiled=True)
    chosen = jnp.take(every_coef, far_cols, axis=0)
    chosen = chosen.reshape(leaf_count, far_count, columns, rank)
    reduced = jnp.einsum("lkra,lakb->lrb", chosen, coupling, preferred_element_type=jnp.float32)
    reduced = reduced.astype(jnp.bfloat16)
    far = jnp.einsum("lrb,lbn->rln", reduced, far_left, preferred_element_type=jnp.float32)
    far = far.reshape(columns, leaf_count * leaf)
    return (near + far).astype(jnp.bfloat16)


def solution(mesh):
    placed = (
        P("group", "cluster"),
        P("cluster", "group", None, None),
        P("cluster", None),
        P("cluster", None, None),
        P("cluster", None, None),
        P("cluster", None, None),
        P("cluster", None),
    )
    return jax.shard_map(
        local, mesh=mesh, in_specs=placed, out_specs=P("group", "cluster"), check_vma=False
    )
```

profile of v0, /device:TPU:1, one launch (start us, length us, event | category | flops | bytes accessed | tf_op | source)
XLA Modules:
  0.0 300.0 jit_solution(17901057089317434044)
XLA Ops:
  6.5 0.0 copy-start
  6.5 0.0 copy-start.3
  6.5 0.0 all-gather.3.cloned.1.call-start
  6.5 0.7 all-gather.3.cloned.1.call-update
  7.3 0.0 all-gather.5.cloned.1.call-start
  7.3 1.5 convolution_convert_fusion
  8.8 0.9 reshape.33
  9.7 0.0 all-gather.5.cloned.1.call-update
  9.8 0.0 reduce-scatter.2.cloned.1.call-start
  9.8 38.2 %all-gather.3.cloned.1.call-done = bf16[512,4096]{1,0:T(8,128)(2,1)} async-done(((bf16[64,4096]{1,0:T(8,128)(2,1)}), bf16[512,4096]{1,0:T(8,128)(2,1)}) %all-gather.3.cloned.1.call-update) | async-done | bytes 4194320 | tf_op jit(solution)/shard_map/all_gather | solution.py:35
  48.0 6.5 %copy.20 = bf16[512,4096]{0,1:T(8,128)(2,1)} copy(bf16[512,4096]{1,0:T(8,128)(2,1)} %all-gather.3.cloned.1.call-done) | data formatting | bytes 8388608 | tf_op jit(solution)/shard_map/all_gather | solution.py:35
  54.4 1.2 collective-permute-start
  55.7 4.0 %collective-permute-start.1 = (bf16[512,4096]{0,1:T(8,128)(2,1)}, bf16[512,4096]{0,1:T(8,128)(2,1)}, u32[]{:S(2)}, u32[]{:S(2)}) collective-permute-start(bf16[512,4096]{0,1:T(8,128)(2,1)} %copy.20), channel_id=1, source_target_pairs={{8,0},{16,8},{24,16},{32,24},{40,32},{48,40},{56,48},{64,56},{72,6... | collective-permute-start | bytes 12582920 | tf_op jit(solution)/shard_map/ppermute | solution.py:18
  59.7 0.0 copy-done.3
  59.7 0.1 compare_and_fusion.1
  59.8 0.1 reshape.38
  59.9 111.9 %collective-permute-done = bf16[512,4096]{0,1:T(8,128)(2,1)} collective-permute-done((bf16[512,4096]{0,1:T(8,128)(2,1)}, bf16[512,4096]{0,1:T(8,128)(2,1)}, u32[]{:S(2)}, u32[]{:S(2)}) %collective-permute-start) | collective-permute-done | bytes 4194336 | tf_op jit(solution)/shard_map/ppermute | solution.py:16
  171.7 0.0 collective-permute-done.1
  171.7 15.9 %pad_maximum_fusion = bf16[512,12288]{0,1:T(8,128)(2,1)} fusion(bf16[512,4096]{0,1:T(8,128)(2,1)} %collective-permute-done.1, bf16[512,4096]{0,1:T(8,128)(2,1)} %copy.20, bf16[512,4096]{0,1:T(8,128)(2,1)} %collective-permute-done), kind=kLoop, calls=%fused_computation.2 | loop fusion | flops 37748736 | bytes 25165824 | tf_op jit(solution)/shard_map/concatenate | solution.py:14
  187.7 15.9 %copy.23 = bf16[512,48,256]{2,0,1:T(8,128)(2,1)} copy(bf16[512,48,256]{0,2,1:T(8,128)(2,1)} %bitcast.29) | data formatting | bytes 25165824 | tf_op jit(solution)/shard_map/reshape | solution.py:39
  203.5 10.9 %gather_fusion = bf16[48,512,256]{2,1,0:T(8,128)(2,1)} fusion(bf16[512,48,256]{2,0,1:T(8,128)(2,1)} %copy.23, s32[1024]{0:T(1024)S(1)} %pad_clamp_fusion.1), kind=kCustom, calls=%fused_computation | custom fusion | bytes 25166016 | tf_op jit(solution)/shard_map/jit(_take)/gather | solution.py:43
  214.4 10.5 %fusion = f32[16,512,256,1]{1,2,3,0:T(8,128)} fusion(bf16[16,3,256,256]{3,2,1,0:T(8,128)(2,1)} %param.8, bf16[16,3,512,256]{3,2,1,0:T(8,128)(2,1)} %bitcast.30, pred[16,3]{1,0:T(8,128)(4,1)S(1)} %get-tuple-element.5), kind=kOutput, calls=%fused_computation.3 | convolution fusion | flops 3227516928 | bytes 27263024 | tf_op jit(solution)/shard_map/rmkc,mknc->rmn/dot_general | solution.py:44
  224.9 8.9 %copy.24 = f32[512,4096]{1,0:T(8,128)} copy(f32[512,4096]{0,1:T(8,128)} %bitcast.31) | data formatting | bytes 16777216 | tf_op jit(solution)/shard_map/reshape | solution.py:45
  233.9 0.0 copy-start.2
  233.9 0.0 copy-start.1
  233.9 0.0 reduce-scatter.2.cloned.1.call-update
  233.9 0.7 copy-done.2
  234.6 0.1 reshape.46
  234.6 0.8 copy-done.1
  235.5 4.1 %reshape.34 = bf16[16,64,16,64]{3,2,1,0:T(8,128)(2,1)} reshape(bf16[16,64,1024]{2,1,0:T(8,128)(2,1)S(1)} %copy-done.1) | data formatting | bytes 4194304 | tf_op jit(solution)/shard_map/reshape | solution.py:50
  239.5 0.0 all-gather.5.cloned.1.call-done
  239.6 6.6 %gather_fusion.1 = bf16[256,4096]{1,0:T(8,128)(2,1)S(1)} fusion(bf16[512,4096]{1,0:T(8,128)(2,1)} %all-gather.5.cloned.1.call-done, s32[1024]{0:T(1024)S(1)} %pad_clamp_fusion), kind=kCustom, calls=%fused_computation.1 | custom fusion | bytes 4195328 | tf_op jit(solution)/shard_map/jit(_take)/gather | solution.py:52
  246.2 5.5 %gather.12 = bf16[16,16,64,64]{3,2,1,0:T(8,128)(2,1)} reshape(bf16[256,4096]{1,0:T(8,128)(2,1)S(1)} %gather_fusion.1) | data formatting | bytes 4194304 | tf_op jit(solution)/shard_map/jit(_take)/gather | solution.py:52
  251.7 0.0 copy-done
  251.7 4.9 %convolution_bitcast_fusion = f32[16,8,8,256]{3,2,1,0:T(8,128)S(1)} fusion(bf16[16,64,256]{2,1,0:T(8,128)(2,1)S(1)} %copy-done, bf16[16,64,16,64]{3,2,1,0:T(8,128)(2,1)} %reshape.34, bf16[16,16,64,64]{3,2,1,0:T(8,128)(2,1)} %gather.12, pred[16,16]{1,0:T(8,128)(4,1)S(1)} %compare_and_fusion), kind=kOutput, calls=%fused_computation.13 | convolution fusion | flops 168886272 | bytes 5767424 | tf_op jit(solution)/shard_map/lrb,lbn->rln/dot_general | solution.py:56
  256.6 0.1 copy.31
  256.7 34.6 %reduce-scatter.2.cloned.1.call-done = f32[64,4096]{1,0:T(8,128)} async-done(((f32[512,4096]{1,0:T(8,128)}), f32[64,4096]{1,0:T(8,128)}) %reduce-scatter.2.cloned.1.call-update) | async-done | bytes 1048592 | tf_op jit(solution)/shard_map/reduce_scatter | solution.py:46
  291.4 2.1 add_convert_fusion
  (4 shorter events, 0.0 us)
Async XLA Ops:
  6.5 245.2 %copy-start = (bf16[16,64,256]{2,1,0:T(8,128)(2,1)S(1)}, bf16[16,64,256]{2,1,0:T(8,128)(2,1)}, u32[]{:S(2)}) copy-start(bf16[16,64,256]{2,1,0:T(8,128)(2,1)} %param.12) | copy-start | bytes 1572868
  6.5 53.1 %copy-start.3 = (s32[16,24]{1,0:T(8,128)S(1)}, s32[16,24]{1,0:T(8,128)}, u32[]{:S(2)}) copy-start(s32[16,24]{1,0:T(8,128)} %param.9) | copy-start | bytes 4612
  6.5 41.5 %all-gather.3.cloned.1.call-start = ((), (), s32[]{:S(2)}) async-start(), calls=%async_computation.1 | async-start | bytes 4718592 | tf_op jit(solution)/shard_map/all_gather | solution.py:35
  7.3 232.3 %all-gather.5.cloned.1.call-start = ((), (), s32[]{:S(2)}) async-start(), calls=%async_computation.3 | async-start | bytes 4325376 | tf_op jit(solution)/shard_map/all_gather | solution.py:51
  9.8 281.6 %reduce-scatter.2.cloned.1.call-start = ((), (), s32[]{:S(2)}) async-start(), calls=%async_computation.2 | async-start | bytes 9437184 | tf_op jit(solution)/shard_map/reduce_scatter | solution.py:46
  54.4 117.3 %collective-permute-start = (bf16[512,4096]{0,1:T(8,128)(2,1)}, bf16[512,4096]{0,1:T(8,128)(2,1)}, u32[]{:S(2)}, u32[]{:S(2)}) collective-permute-start(bf16[512,4096]{0,1:T(8,128)(2,1)} %copy.20), channel_id=1, source_target_pairs={{0,8},{8,16},{16,24},{24,32},{32,40},{40,48},{48,56},{56,64},{64,7... | collective-permute-start | bytes 12582920 | tf_op jit(solution)/shard_map/ppermute | solution.py:16
  55.7 116.1 %collective-permute-start.1 = (bf16[512,4096]{0,1:T(8,128)(2,1)}, bf16[512,4096]{0,1:T(8,128)(2,1)}, u32[]{:S(2)}, u32[]{:S(2)}) collective-permute-start(bf16[512,4096]{0,1:T(8,128)(2,1)} %copy.20), channel_id=1, source_target_pairs={{8,0},{16,8},{24,16},{32,24},{40,32},{48,40},{56,48},{64,56},{72,6... | collective-permute-start | bytes 12582920 | tf_op jit(solution)/shard_map/ppermute | solution.py:18
  233.9 0.7 copy-start.2
  233.9 1.6 copy-start.1
Sparse Core Ops, SparseCore 0:
  9.2 38.7 all-gather.2
  50.6 125.4 all-gather.4
  234.0 57.3 reduce-scatter.1
where the time goes:
time: 301 us; the launch traced here: 300 us
  waiting for transfers between devices  185 us (61%)
  local copies, waits for them, and re-layouts  61 us (20%)
  other arithmetic  18.2 us (6%)
  matrix products  16.9 us (6%)
  between operations  13.2 us (4%)
  starting transfers between devices  5.3 us (2%)
    ppermute x1, waiting for transfers between devices, with_halo(): lax.ppermute(tail, axis, [(i, (i + 1) % count) for i in range(count)])  112 us
    all_gather x1, waiting for transfers between devices, local(): gathered = lax.all_gather(loads, 'group', axis=0, tiled=True)  38.2 us
    reduce_scatter x1, waiting for transfers between devices, local(): lax.psum_scatter(partial_value, 'group', scatter_dimension=0, tiled=True)  34.6 us
    concatenate x1, other arithmetic, with_halo(): jnp.concatenate([lax.ppermute(tail, axis, [(i, (i + 1) % count) for i in...  15.9 us
    reshape x1, local copies, waits for them, and re-layouts, local(): wide_view = widened.reshape(patterns, wide_leaves, leaf)  15.9 us
    gather x2, local copies, waits for them, and re-layouts, local(): chosen = jnp.take(every_coef, far_cols, axis=0)  12.1 us
    gather x1, local copies, waits for them, and re-layouts, local(): picked = jnp.take(wide_view, position, axis=1)  10.9 us
    dot_general x1, matrix products, local(): jnp.einsum('rmkc,mknc->rmn', picked, near_blocks, preferred_element_type=...  10.5 us
  transfers between devices with their start and end apart: 5, of which 3 were waited for; matrix products, arithmetic and copies ran while one was open for 31% of the time, Pallas kernels for 0%

commit v1 on v0

--- a/solution.py
+++ b/solution.py
@@ -32,7 +32,9 @@
     total_leaves = leaf_count * lax.axis_size("cluster")
     cluster_id = lax.axis_index("cluster")
     group_id = lax.axis_index("group")
-    gathered = lax.all_gather(loads, "group", axis=0, tiled=True)
+    gathered = jnp.concatenate(
+        lax.all_to_all(jnp.stack([loads] * lax.axis_size("group")), "group", 0, 0), axis=0
+    )
     patterns = gathered.shape[0]
     widened = with_halo(gathered, (("cluster", 1),), REACH * leaf)
     wide_leaves = leaf_count + 2 * REACH

time: 301 us -> 312 us (1.037)
  local copies, waits for them, and re-layouts: 61 us -> 74.9 us
  starting transfers between devices: 5.3 us -> 14.1 us
  waiting for transfers between devices: 185 us -> 178 us
  other arithmetic: 18.2 us -> 12.9 us
    all_to_all x0 -> x1, waiting for transfers between devices: none -> 47.5 us  [local(): lax.all_to_all(jnp.stack([loads] * lax.axis_size('group')), 'group', 0, 0)]
    all_gather x1 -> x0, waiting for transfers between devices: 38.2 us -> none  [local(): gathered = lax.all_gather(loads, 'group', axis=0, tiled=True)]
    concatenate x0 -> x3, local copies, waits for them, and re-layouts: none -> 16 us  [with_halo(): jnp.concatenate([lax.ppermute(tail, axis, [(i, (i + 1) % count) for i in...]
    reshape x1 -> x0, local copies, waits for them, and re-layouts: 15.9 us -> none  [local(): wide_view = widened.reshape(patterns, wide_leaves, leaf)]
    ppermute x0 -> x2, local copies, waits for them, and re-layouts: none -> 13 us  [the longest x1 6.5 us: with_halo(): lax.ppermute(tail, axis, [(i, (i + 1) % count) for i in range(count)])]
    ppermute x1, waiting for transfers between devices: 112 us -> 103 us  [with_halo(): lax.ppermute(tail, axis, [(i, (i + 1) % count) for i in range(count)])]
    all_to_all x0 -> x1, starting transfers between devices: none -> 7.78 us  [local(): lax.all_to_all(jnp.stack([loads] * lax.axis_size('group')), 'group', 0, 0)]
    reduce_scatter x1, waiting for transfers between devices: 34.6 us -> 27.8 us  [local(): lax.psum_scatter(partial_value, 'group', scatter_dimension=0, tiled=True)]
where the time goes in v1:
time: 312 us; the launch traced here: 311 us
  waiting for transfers between devices  178 us (57%)
  local copies, waits for them, and re-layouts  74.9 us (24%)
  matrix products  15.8 us (5%)
  between operations  14.9 us (5%)
  starting transfers between devices  14.1 us (5%)
  other arithmetic  12.9 us (4%)
    ppermute x1, waiting for transfers between devices, with_halo(): lax.ppermute(tail, axis, [(i, (i + 1) % count) for i in range(count)])  103 us
    all_to_all x1, waiting for transfers between devices, local(): lax.all_to_all(jnp.stack([loads] * lax.axis_size('group')), 'group', 0, 0)  47.5 us
    reduce_scatter x1, waiting for transfers between devices, local(): lax.psum_scatter(partial_value, 'group', scatter_dimension=0, tiled=True)  27.8 us
    concatenate x3, local copies, waits for them, and re-layouts, with_halo(): jnp.concatenate([lax.ppermute(tail, axis, [(i, (i + 1) % count) for i in...  16 us
    gather x2, local copies, waits for them, and re-layouts, local(): chosen = jnp.take(every_coef, far_cols, axis=0)  12.2 us
    gather x1, local copies, waits for them, and re-layouts, local(): picked = jnp.take(wide_view, position, axis=1)  10.8 us
    concatenate x1, other arithmetic, with_halo(): jnp.concatenate([lax.ppermute(tail, axis, [(i, (i + 1) % count) for i in...  10.7 us
    dot_general x1, matrix products, local(): jnp.einsum('rmkc,mknc->rmn', picked, near_blocks, preferred_element_type=...  10.6 us
  transfers between devices with their start and end apart: 5, of which 3 were waited for; matrix products, arithmetic and copies ran while one was open for 31% of the time, Pallas kernels for 0%

profile of v1, /device:TPU:1, one launch (start us, length us, event | category | flops | bytes accessed | tf_op | source)
XLA Modules:
  0.0 310.7 jit_solution(885359490152451527)
XLA Ops:
  7.4 0.0 copy-start
  7.4 3.6 %stack.2 = bf16[8,64,4096]{2,1,0:T(8,128)(2,1)} broadcast(bf16[64,4096]{1,0:T(8,128)(2,1)} %param.7), dimensions={1,2} | broadcast | bytes 4718592 | tf_op jit(solution)/shard_map/stack | solution.py:36
  11.0 0.0 copy-start.2
  11.0 0.0 copy-start.3
  11.0 0.0 copy-start.5
  11.0 7.8 %all-to-all-start = ((bf16[8,64,4096]{2,1,0:T(8,128)(2,1)}), bf16[8,64,4096]{2,1,0:T(8,128)(2,1)}, u32[]{:S(2)}, u32[]{:S(2)}) async-start(bf16[8,64,4096]{2,1,0:T(8,128)(2,1)} %stack.2), calls=%async_computation | async-start | bytes 8388608 | tf_op jit(solution)/shard_map/all_to_all | solution.py:36
  18.8 0.0 all-gather.2.cloned.1.call-start
  18.8 0.0 copy-done.2
  18.8 0.0 copy-done.3
  18.8 0.3 convolution_convert_fusion
  19.1 0.9 reshape.40
  20.0 0.0 all-gather.2.cloned.1.call-update
  20.0 0.0 reduce-scatter.2.cloned.1.call-start
  20.1 47.5 %all-to-all-done = bf16[8,64,4096]{2,1,0:T(8,128)(2,1)} async-done(((bf16[8,64,4096]{2,1,0:T(8,128)(2,1)}), bf16[8,64,4096]{2,1,0:T(8,128)(2,1)}, u32[]{:S(2)}, u32[]{:S(2)}) %all-to-all-start) | async-done | bytes 4194336 | tf_op jit(solution)/shard_map/all_to_all | solution.py:36
  67.6 0.0 collective-permute-start
  67.6 6.3 %collective-permute-start.1 = (bf16[512,4096]{1,0:T(8,128)(2,1)}, bf16[512,4096]{1,0:T(8,128)(2,1)}, u32[]{:S(2)}, u32[]{:S(2)}) collective-permute-start(bf16[512,4096]{1,0:T(8,128)(2,1)} %bitcast), channel_id=1, source_target_pairs={{8,0},{16,8},{24,16},{32,24},{40,32},{48,40},{56,48},{64,56},{72,6... | collective-permute-start | bytes 12582920 | tf_op jit(solution)/shard_map/ppermute | solution.py:18
  73.9 0.0 copy-done.5
  73.9 0.1 compare_and_fusion.1
  74.0 0.1 reshape.45
  74.1 3.6 %copy.34 = bf16[64,8,16,256]{3,2,1,0:T(8,128)(2,1)S(1)} copy(bf16[64,8,16,256]{3,1,2,0:T(8,128)(2,1)} %bitcast.19) | data formatting | bytes 8388608
  77.7 3.5 %copy.24 = bf16[512,16,256]{2,0,1:T(8,128)(2,1)} copy(bf16[512,16,256]{2,1,0:T(8,128)(2,1)S(1)} %bitcast.37) | data formatting | bytes 8388608 | tf_op jit(solution)/shard_map/concatenate | solution.py:14
  81.2 102.7 %collective-permute-done = bf16[512,4096]{1,0:T(8,128)(2,1)} collective-permute-done((bf16[512,4096]{1,0:T(8,128)(2,1)}, bf16[512,4096]{1,0:T(8,128)(2,1)}, u32[]{:S(2)}, u32[]{:S(2)}) %collective-permute-start) | collective-permute-done | bytes 4194336 | tf_op jit(solution)/shard_map/ppermute | solution.py:16
  183.9 6.5 %copy.21 = bf16[512,4096]{0,1:T(8,128)(2,1)} copy(bf16[512,4096]{1,0:T(8,128)(2,1)} %collective-permute-done) | data formatting | bytes 8388608 | tf_op jit(solution)/shard_map/ppermute | solution.py:16
  190.3 6.3 %copy.23 = bf16[512,16,256]{2,0,1:T(8,128)(2,1)} copy(bf16[512,16,256]{0,2,1:T(8,128)(2,1)} %bitcast.35) | data formatting | bytes 8388608 | tf_op jit(solution)/shard_map/concatenate | solution.py:14
  196.6 0.0 collective-permute-done.1
  196.7 6.5 %copy.22 = bf16[512,4096]{0,1:T(8,128)(2,1)} copy(bf16[512,4096]{1,0:T(8,128)(2,1)} %collective-permute-done.1) | data formatting | bytes 8388608 | tf_op jit(solution)/shard_map/ppermute | solution.py:18
  203.1 6.3 %copy.25 = bf16[512,16,256]{2,0,1:T(8,128)(2,1)} copy(bf16[512,16,256]{0,2,1:T(8,128)(2,1)} %bitcast.36) | data formatting | bytes 8388608 | tf_op jit(solution)/shard_map/concatenate | solution.py:14
  209.4 10.7 %pad_maximum_fusion = bf16[512,48,256]{2,0,1:T(8,128)(2,1)} fusion(bf16[512,16,256]{2,0,1:T(8,128)(2,1)} %copy.25, bf16[512,16,256]{2,0,1:T(8,128)(2,1)} %copy.24, bf16[512,16,256]{2,0,1:T(8,128)(2,1)} %copy.23), kind=kLoop, calls=%fused_computation.2 | loop fusion | flops 12582912 | bytes 25165824 | tf_op jit(solution)/shard_map/concatenate | solution.py:14
  220.1 10.8 %gather_fusion = bf16[48,512,256]{2,1,0:T(8,128)(2,1)} fusion(bf16[512,48,256]{2,0,1:T(8,128)(2,1)} %pad_maximum_fusion, s32[1024]{0:T(1024)S(1)} %pad_clamp_fusion.1), kind=kCustom, calls=%fused_computation | custom fusion | bytes 25166016 | tf_op jit(solution)/shard_map/jit(_take)/gather | solution.py:45
  231.0 10.6 %fusion = f32[16,512,256,1]{1,2,3,0:T(8,128)} fusion(bf16[16,3,256,256]{3,2,1,0:T(8,128)(2,1)} %param.8, bf16[16,3,512,256]{3,2,1,0:T(8,128)(2,1)} %bitcast.34, pred[16,3]{1,0:T(8,128)(4,1)S(1)} %get-tuple-element.5), kind=kOutput, calls=%fused_computation.3 | convolution fusion | flops 3227516928 | bytes 27263024 | tf_op jit(solution)/shard_map/rmkc,mknc->rmn/dot_general | solution.py:46
  241.5 8.9 %copy.26 = f32[512,4096]{1,0:T(8,128)} copy(f32[512,4096]{0,1:T(8,128)} %bitcast.38) | data formatting | bytes 16777216 | tf_op jit(solution)/shard_map/reshape | solution.py:47
  250.4 0.0 copy-start.4
  250.4 0.0 copy-start.1
  250.4 0.0 reduce-scatter.2.cloned.1.call-update
  250.5 0.7 copy-done.4
  251.1 0.1 reshape.53
  251.2 0.8 copy-done.1
  252.0 3.9 %reshape.41 = bf16[16,64,16,64]{3,2,1,0:T(8,128)(2,1)} reshape(bf16[16,64,1024]{2,1,0:T(8,128)(2,1)S(1)} %copy-done.1) | data formatting | bytes 4194304 | tf_op jit(solution)/shard_map/reshape | solution.py:52
  256.0 0.0 all-gather.2.cloned.1.call-done
  256.0 6.7 %gather_fusion.1 = bf16[256,4096]{1,0:T(8,128)(2,1)S(1)} fusion(bf16[512,4096]{1,0:T(8,128)(2,1)} %all-gather.2.cloned.1.call-done, s32[1024]{0:T(1024)S(1)} %pad_clamp_fusion), kind=kCustom, calls=%fused_computation.1 | custom fusion | bytes 4195328 | tf_op jit(solution)/shard_map/jit(_take)/gather | solution.py:54
  262.7 5.5 %gather.12 = bf16[16,16,64,64]{3,2,1,0:T(8,128)(2,1)} reshape(bf16[256,4096]{1,0:T(8,128)(2,1)S(1)} %gather_fusion.1) | data formatting | bytes 4194304 | tf_op jit(solution)/shard_map/jit(_take)/gather | solution.py:54
  268.3 0.0 copy-done
  268.3 5.0 %convolution_bitcast_fusion = f32[16,8,8,256]{3,2,1,0:T(8,128)S(1)} fusion(bf16[16,64,256]{2,1,0:T(8,128)(2,1)S(1)} %copy-done, bf16[16,64,16,64]{3,2,1,0:T(8,128)(2,1)} %reshape.41, bf16[16,16,64,64]{3,2,1,0:T(8,128)(2,1)} %gather.12, pred[16,16]{1,0:T(8,128)(4,1)S(1)} %compare_and_fusion), kind=kOutput, calls=%fused_computation.13 | convolution fusion | flops 168886272 | bytes 5767424 | tf_op jit(solution)/shard_map/lrb,lbn->rln/dot_general | solution.py:58
  273.3 0.1 copy.33
  273.4 27.8 %reduce-scatter.2.cloned.1.call-done = f32[64,4096]{1,0:T(8,128)} async-done(((f32[512,4096]{1,0:T(8,128)}), f32[64,4096]{1,0:T(8,128)}) %reduce-scatter.2.cloned.1.call-update) | async-done | bytes 1048592 | tf_op jit(solution)/shard_map/reduce_scatter | solution.py:48
  301.1 2.1 add_convert_fusion
  (4 shorter events, 0.0 us)
Async XLA Ops:
  7.4 260.9 %copy-start = (bf16[16,64,256]{2,1,0:T(8,128)(2,1)S(1)}, bf16[16,64,256]{2,1,0:T(8,128)(2,1)}, u32[]{:S(2)}) copy-start(bf16[16,64,256]{2,1,0:T(8,128)(2,1)} %param.12) | copy-start | bytes 1572868
  11.0 7.8 %copy-start.2 = (bf16[64,4096]{1,0:T(8,128)(2,1)S(1)}, bf16[64,4096]{1,0:T(8,128)(2,1)}, u32[]{:S(2)}) copy-start(bf16[64,4096]{1,0:T(8,128)(2,1)} %param.7) | copy-start | bytes 1572868
  11.0 7.8 %copy-start.3 = (bf16[16,64,256]{2,1,0:T(8,128)(2,1)S(1)}, bf16[16,64,256]{2,1,0:T(8,128)(2,1)}, u32[]{:S(2)}) copy-start(bf16[16,64,256]{2,1,0:T(8,128)(2,1)} %param.10) | copy-start | bytes 1572868
  11.0 62.9 %copy-start.5 = (s32[16,24]{1,0:T(8,128)S(1)}, s32[16,24]{1,0:T(8,128)}, u32[]{:S(2)}) copy-start(s32[16,24]{1,0:T(8,128)} %param.9) | copy-start | bytes 4612
  11.0 56.6 %all-to-all-start = ((bf16[8,64,4096]{2,1,0:T(8,128)(2,1)}), bf16[8,64,4096]{2,1,0:T(8,128)(2,1)}, u32[]{:S(2)}, u32[]{:S(2)}) async-start(bf16[8,64,4096]{2,1,0:T(8,128)(2,1)} %stack.2), calls=%async_computation | async-start | bytes 8388608 | tf_op jit(solution)/shard_map/all_to_all | solution.py:36
  18.8 237.3 %all-gather.2.cloned.1.call-start = ((), (), s32[]{:S(2)}) async-start(), calls=%async_computation.3 | async-start | bytes 4325376 | tf_op jit(solution)/shard_map/all_gather | solution.py:53
  20.0 281.1 %reduce-scatter.2.cloned.1.call-start = ((), (), s32[]{:S(2)}) async-start(), calls=%async_computation.2 | async-start | bytes 9437184 | tf_op jit(solution)/shard_map/reduce_scatter | solution.py:48
  67.6 116.3 %collective-permute-start = (bf16[512,4096]{1,0:T(8,128)(2,1)}, bf16[512,4096]{1,0:T(8,128)(2,1)}, u32[]{:S(2)}, u32[]{:S(2)}) collective-permute-start(bf16[512,4096]{1,0:T(8,128)(2,1)} %bitcast), channel_id=1, source_target_pairs={{0,8},{8,16},{16,24},{24,32},{32,40},{40,48},{48,56},{56,64},{64,7... | collective-permute-start | bytes 12582920 | tf_op jit(solution)/shard_map/ppermute | solution.py:16
  67.6 129.1 %collective-permute-start.1 = (bf16[512,4096]{1,0:T(8,128)(2,1)}, bf16[512,4096]{1,0:T(8,128)(2,1)}, u32[]{:S(2)}, u32[]{:S(2)}) collective-permute-start(bf16[512,4096]{1,0:T(8,128)(2,1)} %bitcast), channel_id=1, source_target_pairs={{8,0},{16,8},{24,16},{32,24},{40,32},{48,40},{56,48},{64,56},{72,6... | collective-permute-start | bytes 12582920 | tf_op jit(solution)/shard_map/ppermute | solution.py:18
  250.4 0.7 copy-start.4
  250.4 1.6 copy-start.1
Sparse Core Ops, SparseCore 0:
  22.1 139.7 all-gather.1
Sparse Core Ops, SparseCore 1:
  250.5 50.5 reduce-scatter.1
